TPU v7x, 32 devices: a whole 2x2x4 slice. The times are simulated.
32 devices in a mesh: group: 2 (over x), dp: 2 (over core), tensor: 8 (over z, y).
Axes of the slice: x: 2, y: 2, z: 4, core: 2. Of those that a mesh axis runs over, the one named last changes fastest.
Arguments:
- teacher_hidden: bfloat16 [1024, 8192], P(('group', 'dp'), 'tensor'), may hold values from -6 to 6
- teacher_gain: float32 [8192], P('tensor'), may hold values from 0.1 to 1.9
- project_weight: bfloat16 [8192, 3584], P('tensor'), may hold values from -0.0625 to 0.0625
- student_hidden: bfloat16 [1024, 3584], P(('group', 'dp', 'tensor')), may hold values from -6 to 6
- student_gain: float32 [3584], replicated, may hold values from 0.1 to 1.9
- gate_weight: bfloat16 [3584, 9472], P(('group', 'dp'), 'tensor'), may hold values from -0.09375 to 0.09375
- up_weight: bfloat16 [3584, 9472], P(('group', 'dp'), 'tensor'), may hold values from -0.09375 to 0.09375
- down_weight: bfloat16 [9472, 3584], P('tensor', ('group', 'dp')), may hold values from -0.0625 to 0.0625
- owner_map: int32 [64, 1], P(('group', 'dp')), may hold values from 0 to 3; in each aligned block of 16 rows (0 to 15, 16 to 31, ...) at most 8 rows name the same one
- token_ids: int32 [1024], P(('group', 'dp', 'tensor')), may hold values from 0 to 511
- token_counts: int32 [64], P(('group', 'dp')), may hold values from 1 to 16
- id_weight: float32 [512], replicated, may hold values from 0.25 to 4
Outputs:
- student_out: bfloat16 [4, 16, 32, 3584], P(('group', 'dp'), 'tensor')
- down_grad: float32 [3584, 9472], P(('group', 'dp'), 'tensor')
Inputs may be any that keep to these rules, and one draw needn't show every extreme that they name: `owner_map`: of the 16 episodes of one index of group and dp (aligned blocks of 16 rows), at most 8 have the same owner; owner o is index o of group and dp in mesh order.
All inputs are finite; a program needn't handle non-finite values.
Results may differ from a plain program's by a relative error of at most 0.02.
Values may be sent and summed in bfloat16 or wider, within the bound.
A program may use at most 128 MiB of HBM per device.

v0:
```python
import math
import jax
import jax.numpy as jnp
from jax import lax
from jax.sharding import PartitionSpec as P

DT = 8192
EP_LEN = 16
EPSILON = 1e-06


def build_selector(owner_local, owners, capacity):
    owner_list = owner_local[:, 0]
    onehot = (owner_list[:, None] == jnp.arange(owners, dtype=jnp.int32)[None, :]).astype(jnp.int32)
    earlier = jnp.cumsum(onehot, axis=0) - onehot
    rank_list = jnp.sum(earlier * onehot, axis=1)
    target = owner_list * capacity + rank_list
    return (target[None, :] == jnp.arange(owners * capacity, dtype=jnp.int32)[:, None]).astype(
        jnp.bfloat16
    )


def dispatch_rows(selector, values):
    return jnp.einsum("re,pef->prf", selector, values, preferred_element_type=jnp.float32).astype(
        jnp.bfloat16
    )


def dispatch_plain(selector, values):
    return jnp.einsum("re,pe->pr", selector, values, preferred_element_type=jnp.float32).astype(
        jnp.bfloat16
    )


def regroup_rows(payload):
    return (
        lax.all_to_all(payload[0], ("group", "dp"), split_axis=1, concat_axis=1, tiled=True),
        lax.all_to_all(payload[1], ("group", "dp"), split_axis=1, concat_axis=1, tiled=True),
        lax.all_to_all(payload[2], ("group", "dp"), split_axis=1, concat_axis=1, tiled=True),
    )


def teacher_scaling(raw_rows, teacher_gain):
    widened = raw_rows.astype(jnp.float32)
    return (
        jnp.sum(widened * widened, axis=1),
        (widened * teacher_gain[None, :]).astype(jnp.bfloat16),
    )


def local(
    teacher_hidden,
    teacher_gain,
    project_weight,
    student_hidden,
    student_gain,
    gate_weight,
    up_weight,
    down_weight,
    owner_map,
    token_ids,
    token_counts,
    id_weight,
):
    groups = lax.axis_size("group")
    places = lax.axis_size("dp")
    owners = groups * places
    tensors = lax.axis_size("tensor")
    tensor_index = lax.axis_index("tensor")
    episodes = token_counts.shape[0]
    own_span = EP_LEN // tensors
    capacity = max(2, 2 * episodes // owners)
    received = owners * capacity
    student_width = student_hidden.shape[1]
    selector = build_selector(owner_map, owners, capacity)
    id_rows = token_ids.reshape(own_span, episodes)
    looked = jnp.sum(
        jnp.where(
            id_rows[:, :, None] == jnp.arange(id_weight.shape[0], dtype=jnp.int32)[None, None, :],
            id_weight[None, None, :],
            0.0,
        ),
        axis=2,
    )
    position = tensor_index * own_span + jnp.arange(own_span, dtype=jnp.int32)[:, None]
    token_weight = jnp.where(position < token_counts[None, :], looked, 0.0).astype(jnp.bfloat16)
    sent_weight = dispatch_plain(selector, token_weight)
    sent_student = dispatch_rows(
        selector, student_hidden.reshape(own_span, episodes, student_width)
    )
    squares, scaled = teacher_scaling(teacher_hidden, teacher_gain)
    totals = lax.psum(squares, "tensor")
    inverse = lax.rsqrt(totals / DT + EPSILON)
    share_rows = own_span * episodes
    summed = lax.psum_scatter(
        jnp.dot(scaled, project_weight, preferred_element_type=jnp.float32).astype(jnp.bfloat16),
        "tensor",
        scatter_dimension=0,
        tiled=True,
    ).astype(jnp.float32)
    own_inverse = lax.dynamic_slice_in_dim(inverse, tensor_index * share_rows, share_rows, 0)
    projected = (
        (summed * own_inverse[:, None])
        .astype(jnp.bfloat16)
        .reshape(own_span, episodes, student_width)
    )
    arrived = regroup_rows((dispatch_rows(selector, projected), sent_student, sent_weight))
    teacher_mine = arrived[0]
    student_block = arrived[1].reshape(own_span * received, student_width).astype(jnp.float32)
    rescale = lax.rsqrt(jnp.mean(student_block * student_block, axis=1, keepdims=True) + EPSILON)
    normed = (student_block * rescale * student_gain[None, :]).astype(jnp.bfloat16)
    gathered = lax.all_gather(normed, "tensor", axis=0, tiled=True)
    gate_sum = jnp.dot(
        gathered,
        lax.all_gather(gate_weight, ("group", "dp"), axis=0, tiled=True),
        preferred_element_type=jnp.float32,
    )
    up_sum = jnp.dot(
        gathered,
        lax.all_gather(up_weight, ("group", "dp"), axis=0, tiled=True),
        preferred_element_type=jnp.float32,
    )
    activated = (jax.nn.silu(gate_sum) * up_sum).astype(jnp.bfloat16)
    branch = jnp.dot(
        activated,
        lax.all_gather(down_weight, ("group", "dp"), axis=1, tiled=True),
        preferred_element_type=jnp.float32,
    )
    branch_local = lax.psum_scatter(
        branch.astype(jnp.bfloat16), "tensor", scatter_dimension=0, tiled=True
    ).astype(jnp.float32)
    predicted = student_block + branch_local
    student_out = predicted.astype(jnp.bfloat16).reshape(1, own_span, received, student_width)
    difference = predicted - teacher_mine.reshape(-1, student_width).astype(jnp.float32)
    weight_rows = arrived[2].reshape(-1, 1).astype(jnp.float32)
    tokens_all = EP_LEN * episodes * owners
    grad_block = (weight_rows * difference * (1.0 / math.sqrt(tokens_all))).astype(jnp.bfloat16)
    grad_all = lax.all_gather(grad_block, "tensor", axis=0, tiled=True)
    down_grad = lax.psum_scatter(
        jnp.einsum("rc,rh->ch", grad_all, activated, preferred_element_type=jnp.float32).astype(
            jnp.bfloat16
        ),
        ("group", "dp"),
        scatter_dimension=0,
        tiled=True,
    ).astype(jnp.float32)
    return (student_out, down_grad)


def solution(mesh):
    in_specs = (
        P(("group", "dp"), "tensor"),
        P("tensor"),
        P("tensor", None),
        P(("group", "dp", "tensor"), None),
        P(),
        P(("group", "dp"), "tensor"),
        P(("group", "dp"), "tensor"),
        P("tensor", ("group", "dp")),
        P(("group", "dp"), None),
        P(("group", "dp", "tensor")),
        P(("group", "dp")),
        P(),
    )
    out_specs = (P(("group", "dp"), "tensor", None, None), P(("group", "dp"), "tensor"))
    return jax.shard_map(local, mesh=mesh, in_specs=in_specs, out_specs=out_specs, check_vma=False)
```

profile of v0, /device:TPU:0, one launch (start us, length us, event | category | flops | bytes accessed | tf_op | source)
XLA Modules:
  0.0 602.6 jit_solution(13602715377556277750)
XLA Ops:
  10.4 12.1 %all_to_all.19 = bf16[2,32,3584]{2,0,1:T(2,128)(2,1)S(1)} all-to-all(bf16[2,32,3584]{2,0,1:T(2,128)(2,1)S(1)} %copy.34), channel_id=1, replica_groups=mesh['group'=2,'dp'=2,'tensor'=8] {'group','dp'}, dimensions={1} | all-to-all | bytes 917504 | tf_op jit(solution)/shard_map/all_to_all | solution.py:38
  22.8 1.7 fusion.10
  26.7 6.4 %convolution_convert_fusion.2 = bf16[256,3584]{1,0:T(8,128)(2,1)} fusion(bf16[1024,3584]{1,0:T(8,128)(2,1)} %param.14, bf16[256,1024]{1,0:T(8,128)(2,1)S(1)} %copy-done.2, f32[1024]{0:T(1024)S(1)} %copy-done.4), kind=kOutput, calls=%fused_computation.2 | convolution fusion | flops 1880752128 | bytes 9703424 | tf_op jit(solution)/shard_map/dot_general | solution.py:96
  33.2 58.1 %all-gather.6.cloned.1.call-done = bf16[512,3584]{1,0:T(8,128)(2,1)} async-done(((bf16[64,3584]{1,0:T(8,128)(2,1)}), bf16[512,3584]{1,0:T(8,128)(2,1)}) %all-gather.6.cloned.1.call-update) | async-done | bytes 3670032 | tf_op jit(solution)/shard_map/all_gather | solution.py:112
  91.3 59.1 %all-gather.8.cloned.1.call-done = bf16[3584,1184]{0,1:T(8,128)(2,1)} async-done(((bf16[896,1184]{0,1:T(8,128)(2,1)}), bf16[3584,1184]{0,1:T(8,128)(2,1)}) %all-gather.8.cloned.1.call-update) | async-done | bytes 8486928 | tf_op jit(solution)/shard_map/all_gather | solution.py:115
  150.4 10.6 %fusion.27 = f32[512,1184]{0,1:T(8,128)} fusion(bf16[512,3584]{1,0:T(8,128)(2,1)} %all-gather.6.cloned.1.call-done, bf16[3584,1184]{0,1:T(8,128)(2,1)} %all-gather.8.cloned.1.call-done), kind=kOutput, calls=%fused_computation.48 | convolution fusion | flops 4345298944 | bytes 14581760 | tf_op jit(solution)/shard_map/dot_general | solution.py:113
  160.9 49.8 %all-gather.10.cloned.1.call-done = bf16[3584,1184]{0,1:T(8,128)(2,1)} async-done(((bf16[896,1184]{0,1:T(8,128)(2,1)}), bf16[3584,1184]{0,1:T(8,128)(2,1)}) %all-gather.10.cloned.1.call-update) | async-done | bytes 8486928 | tf_op jit(solution)/shard_map/all_gather | solution.py:120
  210.7 10.0 %fusion.2 = bf16[512,1184]{0,1:T(8,128)(2,1)S(1)} fusion(bf16[512,3584]{1,0:T(8,128)(2,1)} %all-gather.6.cloned.1.call-done, bf16[3584,1184]{0,1:T(8,128)(2,1)} %all-gather.10.cloned.1.call-done, f32[512,1184]{0,1:T(8,128)} %fusion.27), kind=kOutput, calls=%fused_computation.8 | convolution fusion | flops 4348936192 | bytes 15794176 | tf_op jit(solution)/shard_map/dot_general | solution.py:118
  220.8 50.2 %all-gather.12.cloned.1.call-done = bf16[1184,3584]{1,0:T(8,128)(2,1)} async-done(((bf16[1184,896]{1,0:T(8,128)(2,1)}), bf16[1184,3584]{1,0:T(8,128)(2,1)}) %all-gather.12.cloned.1.call-update) | async-done | bytes 8486928 | tf_op jit(solution)/shard_map/all_gather | solution.py:126
  270.9 9.8 %convolution_convert_fusion.1 = bf16[512,3584]{1,0:T(8,128)(2,1)} fusion(bf16[512,1184]{0,1:T(8,128)(2,1)S(1)} %fusion.2, bf16[1184,3584]{1,0:T(8,128)(2,1)} %all-gather.12.cloned.1.call-done), kind=kOutput, calls=%fused_computation.1 | convolution fusion | flops 4347133952 | bytes 13369344 | tf_op jit(solution)/shard_map/dot_general | solution.py:124
  282.5 3.2 all-to-all-start.1
  286.0 21.6 %psum.7 = f32[256]{0:T(256)S(1)} all-reduce(f32[256]{0:T(256)S(1)} %fusion.4), channel_id=1, replica_groups=mesh['group'=2,'dp'=2,'tensor'=8] {'tensor'}, use_global_device_ids=true, to_apply=%region_7.8 | all-reduce | flops 256 | bytes 2048 | tf_op jit(solution)/shard_map/psum | solution.py:92
  307.6 33.5 %reduce-scatter.8.cloned.1.call-done = bf16[32,3584]{1,0:T(8,128)(2,1)} async-done(((bf16[256,3584]{1,0:T(8,128)(2,1)}), bf16[32,3584]{1,0:T(8,128)(2,1)}) %reduce-scatter.8.cloned.1.call-update) | async-done | bytes 229392 | tf_op jit(solution)/shard_map/reduce_scatter | solution.py:95
  342.6 1.2 copy.40
  343.8 3.5 all-to-all-start.2
  347.5 7.9 %all-to-all-done.2 = bf16[2,32,3584]{2,0,1:T(2,128)(2,1)S(1)} async-done(((bf16[2,32,3584]{2,0,1:T(2,128)(2,1)}), bf16[2,32,3584]{2,0,1:T(2,128)(2,1)S(1)}, u32[]{:S(2)}, u32[]{:S(2)}) %all-to-all-start.2) | async-done | bytes 458784 | tf_op jit(solution)/shard_map/all_to_all | solution.py:37
  355.4 69.6 %reduce-scatter.6.cloned.1.call-done = bf16[64,3584]{1,0:T(8,128)(2,1)} async-done(((bf16[512,3584]{1,0:T(8,128)(2,1)}), bf16[64,3584]{1,0:T(8,128)(2,1)}) %reduce-scatter.6.cloned.1.call-update) | async-done | bytes 458768 | tf_op jit(solution)/shard_map/reduce_scatter | solution.py:129
  425.0 2.1 fusion.7
  427.3 66.6 %all-gather.14.cloned.1.call-done = bf16[512,3584]{1,0:T(8,128)(2,1)} async-done(((bf16[64,3584]{1,0:T(8,128)(2,1)}), bf16[512,3584]{1,0:T(8,128)(2,1)}) %all-gather.14.cloned.1.call-update) | async-done | bytes 3670032 | tf_op jit(solution)/shard_map/all_gather | solution.py:138
  493.8 8.7 %convolution_convert_fusion = bf16[3584,1184]{0,1:T(8,128)(2,1)} fusion(bf16[512,1184]{0,1:T(8,128)(2,1)S(1)} %fusion.2, bf16[512,3584]{1,0:T(8,128)(2,1)} %all-gather.14.cloned.1.call-done), kind=kOutput, calls=%fused_computation | convolution fusion | flops 4349542400 | bytes 13369344 | tf_op jit(solution)/shard_map/rc,rh->ch/dot_general | solution.py:140
  502.6 12.6 %copy.42 = bf16[3584,1184]{1,0:T(8,128)(2,1)} copy(bf16[3584,1184]{0,1:T(8,128)(2,1)} %convolution_convert_fusion) | data formatting | bytes 16973824
  515.2 75.1 %reduce-scatter.10.cloned.1.call-done = bf16[896,1184]{1,0:T(8,128)(2,1)} async-done(((bf16[3584,1184]{1,0:T(8,128)(2,1)}), bf16[896,1184]{1,0:T(8,128)(2,1)}) %reduce-scatter.10.cloned.1.call-update) | async-done | bytes 2121744
  590.3 3.2 copy.43
  593.5 2.3 convert_element_type.113
  (54 shorter events, 9.3 us)
Async XLA Ops:
  7.2 2.4 copy-start
  7.2 84.1 %all-gather.6.cloned.1.call-start = ((), (), s32[]{:S(2)}) async-start(), calls=%async_computation.6 | async-start | bytes 4128768 | tf_op jit(solution)/shard_map/all_gather | solution.py:112
  22.8 3.9 copy-start.2
  22.8 3.9 copy-start.4
  24.6 125.8 %all-gather.8.cloned.1.call-start = ((), (), s32[]{:S(2)}) async-start(), calls=%async_computation.7 | async-start | bytes 10608640 | tf_op jit(solution)/shard_map/all_gather | solution.py:115
  25.3 185.4 %all-gather.10.cloned.1.call-start = ((), (), s32[]{:S(2)}) async-start(), calls=%async_computation.8 | async-start | bytes 10608640 | tf_op jit(solution)/shard_map/all_gather | solution.py:120
  26.1 244.9 %all-gather.12.cloned.1.call-start = ((), (), s32[]{:S(2)}) async-start(), calls=%async_computation.9 | async-start | bytes 10608640 | tf_op jit(solution)/shard_map/all_gather | solution.py:126
  26.6 314.5 %reduce-scatter.8.cloned.1.call-start = ((), (), s32[]{:S(2)}) async-start(), calls=%async_computation.11 | async-start | bytes 2064384 | tf_op jit(solution)/shard_map/reduce_scatter | solution.py:95
  33.1 391.9 %reduce-scatter.6.cloned.1.call-start = ((), (), s32[]{:S(2)}) async-start(), calls=%async_computation.10 | async-start | bytes 4128768 | tf_op jit(solution)/shard_map/reduce_scatter | solution.py:129
  280.8 0.7 copy-start.5
  280.8 0.7 copy-start.3
  280.8 0.9 copy-start.6
  282.5 61.3 %all-to-all-start.1 = ((bf16[2,4,8]{2,0,1:T(2,128)(2,1)}), bf16[2,4,8]{2,0,1:T(2,128)(2,1)S(1)}, u32[]{:S(2)}, u32[]{:S(2)}) async-start(bf16[2,4,8]{2,0,1:T(2,128)(2,1)} %copy.38), calls=%async_computation.2 | async-start | bytes 4096 | tf_op jit(solution)/shard_map/all_to_all | solution.py:39
  343.8 11.6 %all-to-all-start.2 = ((bf16[2,32,3584]{2,0,1:T(2,128)(2,1)}), bf16[2,32,3584]{2,0,1:T(2,128)(2,1)S(1)}, u32[]{:S(2)}, u32[]{:S(2)}) async-start(bf16[2,32,3584]{2,0,1:T(2,128)(2,1)} %copy.40), calls=%async_computation.4 | async-start | bytes 917504 | tf_op jit(solution)/shard_map/all_to_all | solution.py:37
  347.3 146.5 %all-gather.14.cloned.1.call-start = ((), (), s32[]{:S(2)}) async-start(), calls=%async_computation.12 | async-start | bytes 4128768 | tf_op jit(solution)/shard_map/all_gather | solution.py:138
  427.2 163.1 %reduce-scatter.10.cloned.1.call-start = ((), (), s32[]{:S(2)}) async-start(), calls=%async_computation.13 | async-start | bytes 11468800
  590.3 5.5 copy-start.1
Sparse Core Ops, SparseCore 0:
  24.7 66.5 all-gather.5
  92.8 57.4 all-gather.7
  151.9 58.7 all-gather.9
  212.1 58.7 all-gather.11
  274.3 66.8 reduce-scatter.7
  345.2 79.7 reduce-scatter.5
  427.8 65.9 all-gather.13
  515.3 74.9 reduce-scatter.9
where the time goes:
time: 604 us; the launch traced here: 603 us
  waiting for transfers between devices  472 us (78%)
  matrix products  46.5 us (8%)
  blocking collectives  33.7 us (6%)
  local copies, waits for them, and re-layouts  19.2 us (3%)
  between operations  14.3 us (2%)
  other arithmetic  10.1 us (2%)
  starting transfers between devices  7.01 us (1%)
    unnamed x9, waiting for transfers between devices  77.1 us
    reduce_scatter x1, waiting for transfers between devices, local(): lax.psum_scatter(branch.astype(jnp.bfloat16), 'tensor', scatter_dimension...  69.6 us
    all_gather x1, waiting for transfers between devices, local(): grad_all = lax.all_gather(grad_block, 'tensor', axis=0, tiled=True)  66.6 us
    all_gather x1, waiting for transfers between devices, local(): lax.all_gather(gate_weight, ('group', 'dp'), axis=0, tiled=True)  59.1 us
    all_gather x1, waiting for transfers between devices, local(): gathered = lax.all_gather(normed, 'tensor', axis=0, tiled=True)  58.1 us
    all_gather x1, waiting for transfers between devices, local(): lax.all_gather(down_weight, ('group', 'dp'), axis=1, tiled=True)  50.2 us
    all_gather x1, waiting for transfers between devices, local(): lax.all_gather(up_weight, ('group', 'dp'), axis=0, tiled=True)  49.8 us
    reduce_scatter x1, waiting for transfers between devices, local(): lax.psum_scatter(jnp.dot(scaled, project_weight, preferred_element_type=j...  33.5 us
  transfers between devices with their start and end apart: 10, of which 9 were waited for; matrix products, arithmetic and copies ran while one was open for 7% of the time, Pallas kernels for 0%

commit v1 on v0

--- a/solution.py
+++ b/solution.py
@@ -7,6 +7,16 @@
 DT = 8192
 EP_LEN = 16
 EPSILON = 1e-06
+
+
+def turned_line(array, axis, dim):
+    count = lax.axis_size(axis)
+    block, pieces = (array, [array])
+    for _ in range(count - 1):
+        block = lax.ppermute(block, axis, [(i, (i + 1) % count) for i in range(count)])
+        pieces.insert(0, block)
+    row_of_blocks = jnp.concatenate(pieces, axis=dim)
+    return jnp.roll(row_of_blocks, (lax.axis_index(axis) + 1) * array.shape[dim], axis=dim)
 
 
 def build_selector(owner_local, owners, capacity):
@@ -109,7 +119,7 @@
     student_block = arrived[1].reshape(own_span * received, student_width).astype(jnp.float32)
     rescale = lax.rsqrt(jnp.mean(student_block * student_block, axis=1, keepdims=True) + EPSILON)
     normed = (student_block * rescale * student_gain[None, :]).astype(jnp.bfloat16)
-    gathered = lax.all_gather(normed, "tensor", axis=0, tiled=True)
+    gathered = turned_line(normed, "tensor", 0)
     gate_sum = jnp.dot(
         gathered,
         lax.all_gather(gate_weight, ("group", "dp"), axis=0, tiled=True),

time: 604 us -> 464 us (0.77)
  waiting for transfers between devices: 472 us -> 310 us
  local copies, waits for them, and re-layouts: 19.2 us -> 35.6 us
    ppermute x0 -> x7, waiting for transfers between devices: none -> 81.3 us  [turned_line(): lax.ppermute(block, axis, [(i, (i + 1) % count) for i in range(count)])]
    all_gather x1, waiting for transfers between devices: 59.1 us -> 0.01 us  [local(): lax.all_gather(gate_weight, ('group', 'dp'), axis=0, tiled=True)]
    all_gather x1 -> x0, waiting for transfers between devices: 58.1 us -> none  [local(): gathered = lax.all_gather(normed, 'tensor', axis=0, tiled=True)]
    all_gather x1, waiting for transfers between devices: 49.8 us -> 0.01 us  [local(): lax.all_gather(up_weight, ('group', 'dp'), axis=0, tiled=True)]
    reduce_scatter x1, waiting for transfers between devices: 33.5 us -> 0.01 us  [local(): lax.psum_scatter(jnp.dot(scaled, project_weight, preferred_element_type=j...]
    reduce_scatter x1, waiting for transfers between devices: 69.6 us -> 40.1 us  [local(): lax.psum_scatter(branch.astype(jnp.bfloat16), 'tensor', scatter_dimension...]
    unnamed x16 -> x33, local copies, waits for them, and re-layouts: 16.4 us -> 32.1 us
    all_gather x1, waiting for transfers between devices: 50.2 us -> 37.4 us  [local(): lax.all_gather(down_weight, ('group', 'dp'), axis=1, tiled=True)]
  transfers between devices with their start and end apart: 10 -> 16, of which waited for: 9 -> 12; matrix products, arithmetic and copies ran while one was open for 7% -> 14% of each run, Pallas kernels for 0% -> 0%
where the time goes in v1:
time: 464 us; the launch traced here: 463 us
  waiting for transfers between devices  310 us (67%)
  matrix products  48.1 us (10%)
  blocking collectives  35.8 us (8%)
  local copies, waits for them, and re-layouts  35.6 us (8%)
  between operations  15.7 us (3%)
  starting transfers between devices  8.96 us (2%)
  other arithmetic  8.49 us (2%)
    ppermute x7, waiting for transfers between devices, turned_line(): lax.ppermute(block, axis, [(i, (i + 1) % count) for i in range(count)])  81.3 us
    unnamed x8, waiting for transfers between devices  77.3 us
    all_gather x1, waiting for transfers between devices, local(): grad_all = lax.all_gather(grad_block, 'tensor', axis=0, tiled=True)  66 us
    reduce_scatter x1, waiting for transfers between devices, local(): lax.psum_scatter(branch.astype(jnp.bfloat16), 'tensor', scatter_dimension...  40.1 us
    all_gather x1, waiting for transfers between devices, local(): lax.all_gather(down_weight, ('group', 'dp'), axis=1, tiled=True)  37.4 us
    unnamed x33, local copies, waits for them, and re-layouts  32.1 us
    psum x1, blocking collectives, local(): totals = lax.psum(squares, 'tensor')  22.3 us
    all_to_all x1, blocking collectives, regroup_rows(): lax.all_to_all(payload[1], ('group', 'dp'), split_axis=1, concat_axis=1,...  13.5 us
  transfers between devices with their start and end apart: 16, of which 12 were waited for; matrix products, arithmetic and copies ran while one was open for 14% of the time, Pallas kernels for 0%

profile of v1, /device:TPU:0, one launch (start us, length us, event | category | flops | bytes accessed | tf_op | source)
XLA Modules:
  0.0 462.7 jit_solution(4166339590388104431)
XLA Ops:
  13.4 13.5 %all_to_all.19 = bf16[2,32,3584]{2,0,1:T(2,128)(2,1)S(1)} all-to-all(bf16[2,32,3584]{2,0,1:T(2,128)(2,1)S(1)} %copy.34), channel_id=1, replica_groups=mesh['group'=2,'dp'=2,'tensor'=8] {'group','dp'}, dimensions={1} | all-to-all | bytes 917504 | tf_op jit(solution)/shard_map/all_to_all | solution.py:48
  29.1 13.7 %collective-permute-done = bf16[64,3584]{1,0:T(8,128)(2,1)S(1)} collective-permute-done((bf16[64,3584]{1,0:T(8,128)(2,1)S(1)}, bf16[64,3584]{1,0:T(8,128)(2,1)S(1)}, u32[]{:S(2)}, u32[]{:S(2)}) %collective-permute-start) | collective-permute-done | bytes 458784 | tf_op jit(solution)/shard_map/ppermute | solution.py:16
  42.7 14.2 %collective-permute-done.1 = bf16[64,3584]{1,0:T(8,128)(2,1)S(1)} collective-permute-done((bf16[64,3584]{1,0:T(8,128)(2,1)S(1)}, bf16[64,3584]{1,0:T(8,128)(2,1)S(1)}, u32[]{:S(2)}, u32[]{:S(2)}) %collective-permute-start.1) | collective-permute-done | bytes 458784 | tf_op jit(solution)/shard_map/ppermute | solution.py:16
  57.0 13.4 %collective-permute-done.2 = bf16[64,3584]{1,0:T(8,128)(2,1)S(1)} collective-permute-done((bf16[64,3584]{1,0:T(8,128)(2,1)S(1)}, bf16[64,3584]{1,0:T(8,128)(2,1)S(1)}, u32[]{:S(2)}, u32[]{:S(2)}) %collective-permute-start.2) | collective-permute-done | bytes 458784 | tf_op jit(solution)/shard_map/ppermute | solution.py:16
  70.4 12.5 %collective-permute-done.3 = bf16[64,3584]{1,0:T(8,128)(2,1)S(1)} collective-permute-done((bf16[64,3584]{1,0:T(8,128)(2,1)S(1)}, bf16[64,3584]{1,0:T(8,128)(2,1)S(1)}, u32[]{:S(2)}, u32[]{:S(2)}) %collective-permute-start.3) | collective-permute-done | bytes 458784 | tf_op jit(solution)/shard_map/ppermute | solution.py:16
  82.9 11.7 %collective-permute-done.4 = bf16[64,3584]{1,0:T(8,128)(2,1)S(1)} collective-permute-done((bf16[64,3584]{1,0:T(8,128)(2,1)S(1)}, bf16[64,3584]{1,0:T(8,128)(2,1)S(1)}, u32[]{:S(2)}, u32[]{:S(2)}) %collective-permute-start.4) | collective-permute-done | bytes 458784 | tf_op jit(solution)/shard_map/ppermute | solution.py:16
  94.6 11.3 %collective-permute-done.5 = bf16[64,3584]{1,0:T(8,128)(2,1)} collective-permute-done((bf16[64,3584]{1,0:T(8,128)(2,1)S(1)}, bf16[64,3584]{1,0:T(8,128)(2,1)}, u32[]{:S(2)}, u32[]{:S(2)}) %collective-permute-start.5) | collective-permute-done | bytes 458784 | tf_op jit(solution)/shard_map/ppermute | solution.py:16
  105.8 6.7 %convolution_convert_fusion.2 = bf16[256,3584]{1,0:T(8,128)(2,1)} fusion(bf16[1024,3584]{1,0:T(8,128)(2,1)} %param.14, bf16[256,1024]{1,0:T(8,128)(2,1)} %param.12, f32[1024]{0:T(1024)S(1)} %copy-done.5), kind=kOutput, calls=%fused_computation.2 | convolution fusion | flops 1880752128 | bytes 9703424 | tf_op jit(solution)/shard_map/dot_general | solution.py:106
  112.8 4.5 collective-permute-done.6
  134.5 10.6 %fusion.4 = f32[512,1184]{0,1:T(8,128)} fusion(bf16[3584,1184]{0,1:T(8,128)(2,1)} %all-gather.5.cloned.1.call-done, bf16[1024,3584]{1,0:T(8,128)(2,1)} %constant_dynamic-update-slice_fusion, s32[]{:T(128)S(6)} %select_n.25), kind=kOutput, calls=%fused_computation.9 | convolution fusion | flops 4345298944 | bytes 14581764 | tf_op jit(solution)/shard_map/dot_general | solution.py:123
  145.1 11.3 %multiply_convert_fusion = bf16[512,1184]{0,1:T(8,128)(2,1)S(1)} fusion(f32[512,1184]{0,1:T(8,128)} %fusion.4, bf16[3584,1184]{0,1:T(8,128)(2,1)} %all-gather.7.cloned.1.call-done, bf16[1024,3584]{1,0:T(8,128)(2,1)} %constant_dynamic-update-slice_fusion, s32[]{:T(128)S(6)} %select_n.25), kind=kOutput, calls=%fused_computation.11 | convolution fusion | flops 4348936192 | bytes 15794180 | tf_op jit(solution)/shard_map/dot_general | solution.py:128
  156.5 37.4 %all-gather.9.cloned.1.call-done = bf16[1184,3584]{1,0:T(8,128)(2,1)} async-done(((bf16[1184,896]{1,0:T(8,128)(2,1)}), bf16[1184,3584]{1,0:T(8,128)(2,1)}) %all-gather.9.cloned.1.call-update) | async-done | bytes 8486928 | tf_op jit(solution)/shard_map/all_gather | solution.py:136
  193.8 9.8 %convolution_convert_fusion.1 = bf16[512,3584]{1,0:T(8,128)(2,1)} fusion(bf16[512,1184]{0,1:T(8,128)(2,1)S(1)} %multiply_convert_fusion, bf16[1184,3584]{1,0:T(8,128)(2,1)} %all-gather.9.cloned.1.call-done), kind=kOutput, calls=%fused_computation.1 | convolution fusion | flops 4347133952 | bytes 13369344 | tf_op jit(solution)/shard_map/dot_general | solution.py:134
  204.8 3.2 all-to-all-start.1
  208.1 22.3 %psum.7 = f32[256]{0:T(256)S(1)} all-reduce(f32[256]{0:T(256)S(1)} %fusion.7), channel_id=1, replica_groups=mesh['group'=2,'dp'=2,'tensor'=8] {'tensor'}, use_global_device_ids=true, to_apply=%region_7.8 | all-reduce | flops 256 | bytes 2048 | tf_op jit(solution)/shard_map/psum | solution.py:102
  233.2 3.5 all-to-all-start.2
  236.8 7.9 %all-to-all-done.2 = bf16[2,32,3584]{2,0,1:T(2,128)(2,1)S(1)} async-done(((bf16[2,32,3584]{2,0,1:T(2,128)(2,1)}), bf16[2,32,3584]{2,0,1:T(2,128)(2,1)S(1)}, u32[]{:S(2)}, u32[]{:S(2)}) %all-to-all-start.2) | async-done | bytes 458784 | tf_op jit(solution)/shard_map/all_to_all | solution.py:47
  244.8 40.1 %reduce-scatter.6.cloned.1.call-done = bf16[64,3584]{1,0:T(8,128)(2,1)} async-done(((bf16[512,3584]{1,0:T(8,128)(2,1)}), bf16[64,3584]{1,0:T(8,128)(2,1)}) %reduce-scatter.6.cloned.1.call-update) | async-done | bytes 458768 | tf_op jit(solution)/shard_map/reduce_scatter | solution.py:139
  287.4 66.0 %all-gather.11.cloned.1.call-done = bf16[512,3584]{1,0:T(8,128)(2,1)} async-done(((bf16[64,3584]{1,0:T(8,128)(2,1)}), bf16[512,3584]{1,0:T(8,128)(2,1)}) %all-gather.11.cloned.1.call-update) | async-done | bytes 3670032 | tf_op jit(solution)/shard_map/all_gather | solution.py:148
  353.4 8.8 %convolution_convert_fusion = bf16[3584,1184]{0,1:T(8,128)(2,1)} fusion(bf16[512,1184]{0,1:T(8,128)(2,1)S(1)} %multiply_convert_fusion, bf16[512,3584]{1,0:T(8,128)(2,1)} %all-gather.11.cloned.1.call-done), kind=kOutput, calls=%fused_computation | convolution fusion | flops 4349542400 | bytes 13369344 | tf_op jit(solution)/shard_map/rc,rh->ch/dot_general | solution.py:150
  362.2 12.6 %copy.42 = bf16[3584,1184]{1,0:T(8,128)(2,1)} copy(bf16[3584,1184]{0,1:T(8,128)(2,1)} %convolution_convert_fusion) | data formatting | bytes 16973824
  374.8 75.2 %reduce-scatter.10.cloned.1.call-done = bf16[896,1184]{1,0:T(8,128)(2,1)} async-done(((bf16[3584,1184]{1,0:T(8,128)(2,1)}), bf16[896,1184]{1,0:T(8,128)(2,1)}) %reduce-scatter.10.cloned.1.call-update) | async-done | bytes 2121744
  450.0 3.1 copy.43
  453.1 2.3 convert_element_type.113
  (83 shorter events, 31.5 us)
Async XLA Ops:
  8.0 4.6 copy-start
  8.0 19.2 %copy-start.3 = (f32[3584]{0:T(1024)S(1)}, f32[3584]{0:T(1024)}, u32[]{:S(2)}) copy-start(f32[3584]{0:T(1024)} %param.16) | copy-start | bytes 43012
  8.0 97.8 %copy-start.5 = (f32[1024]{0:T(1024)S(1)}, f32[1024]{0:T(1024)}, u32[]{:S(2)}) copy-start(f32[1024]{0:T(1024)} %param.13) | copy-start | bytes 12292
  8.0 126.4 %all-gather.5.cloned.1.call-start = ((), (), s32[]{:S(2)}) async-start(), calls=%async_computation.6 | async-start | bytes 10608640 | tf_op jit(solution)/shard_map/all_gather | solution.py:125
  8.8 136.3 %all-gather.7.cloned.1.call-start = ((), (), s32[]{:S(2)}) async-start(), calls=%async_computation.7 | async-start | bytes 10608640 | tf_op jit(solution)/shard_map/all_gather | solution.py:130
  9.5 184.3 %all-gather.9.cloned.1.call-start = ((), (), s32[]{:S(2)}) async-start(), calls=%async_computation.8 | async-start | bytes 10608640 | tf_op jit(solution)/shard_map/all_gather | solution.py:136
  10.3 220.2 %reduce-scatter.8.cloned.1.call-start = ((), (), s32[]{:S(2)}) async-start(), calls=%async_computation.10 | async-start | bytes 2064384 | tf_op jit(solution)/shard_map/reduce_scatter | solution.py:105
  27.4 15.3 %collective-permute-start = (bf16[64,3584]{1,0:T(8,128)(2,1)S(1)}, bf16[64,3584]{1,0:T(8,128)(2,1)S(1)}, u32[]{:S(2)}, u32[]{:S(2)}) collective-permute-start(bf16[64,3584]{1,0:T(8,128)(2,1)S(1)} %fusion.13), channel_id=1, source_target_pairs={{0,1},{1,2},{2,3},{3,4},{4,5},{5,6},{6,7},{7,0},{8,9},{9,10},{10,1... | collective-permute-start | bytes 1376264 | tf_op jit(solution)/shard_map/ppermute | solution.py:16
  42.7 14.2 %collective-permute-start.1 = (bf16[64,3584]{1,0:T(8,128)(2,1)S(1)}, bf16[64,3584]{1,0:T(8,128)(2,1)S(1)}, u32[]{:S(2)}, u32[]{:S(2)}) collective-permute-start(bf16[64,3584]{1,0:T(8,128)(2,1)S(1)} %collective-permute-done), channel_id=1, source_target_pairs={{0,1},{1,2},{2,3},{3,4},{4,5},{5,6},{6,7},{7,0},{8,9},{9,10},{10,1... | collective-permute-start | bytes 1376264 | tf_op jit(solution)/shard_map/ppermute | solution.py:16
  57.0 13.4 %collective-permute-start.2 = (bf16[64,3584]{1,0:T(8,128)(2,1)S(1)}, bf16[64,3584]{1,0:T(8,128)(2,1)S(1)}, u32[]{:S(2)}, u32[]{:S(2)}) collective-permute-start(bf16[64,3584]{1,0:T(8,128)(2,1)S(1)} %collective-permute-done.1), channel_id=1, source_target_pairs={{0,1},{1,2},{2,3},{3,4},{4,5},{5,6},{6,7},{7,0},{8,9},{9,10},{10,1... | collective-permute-start | bytes 1376264 | tf_op jit(solution)/shard_map/ppermute | solution.py:16
  70.4 12.5 %collective-permute-start.3 = (bf16[64,3584]{1,0:T(8,128)(2,1)S(1)}, bf16[64,3584]{1,0:T(8,128)(2,1)S(1)}, u32[]{:S(2)}, u32[]{:S(2)}) collective-permute-start(bf16[64,3584]{1,0:T(8,128)(2,1)S(1)} %collective-permute-done.2), channel_id=1, source_target_pairs={{0,1},{1,2},{2,3},{3,4},{4,5},{5,6},{6,7},{7,0},{8,9},{9,10},{10,1... | collective-permute-start | bytes 1376264 | tf_op jit(solution)/shard_map/ppermute | solution.py:16
  82.9 11.7 %collective-permute-start.4 = (bf16[64,3584]{1,0:T(8,128)(2,1)S(1)}, bf16[64,3584]{1,0:T(8,128)(2,1)S(1)}, u32[]{:S(2)}, u32[]{:S(2)}) collective-permute-start(bf16[64,3584]{1,0:T(8,128)(2,1)S(1)} %collective-permute-done.3), channel_id=1, source_target_pairs={{0,1},{1,2},{2,3},{3,4},{4,5},{5,6},{6,7},{7,0},{8,9},{9,10},{10,1... | collective-permute-start | bytes 1376264 | tf_op jit(solution)/shard_map/ppermute | solution.py:16
  94.6 11.3 %collective-permute-start.5 = (bf16[64,3584]{1,0:T(8,128)(2,1)S(1)}, bf16[64,3584]{1,0:T(8,128)(2,1)}, u32[]{:S(2)}, u32[]{:S(2)}) collective-permute-start(bf16[64,3584]{1,0:T(8,128)(2,1)S(1)} %collective-permute-done.4), channel_id=1, source_target_pairs={{0,1},{1,2},{2,3},{3,4},{4,5},{5,6},{6,7},{7,0},{8,9},{9,10},{10,1... | collective-permute-start | bytes 1376264 | tf_op jit(solution)/shard_map/ppermute | solution.py:16
  105.8 11.5 %collective-permute-start.6 = (bf16[64,3584]{1,0:T(8,128)(2,1)}, bf16[64,3584]{1,0:T(8,128)(2,1)}, u32[]{:S(2)}, u32[]{:S(2)}) collective-permute-start(bf16[64,3584]{1,0:T(8,128)(2,1)} %collective-permute-done.5), channel_id=1, source_target_pairs={{0,1},{1,2},{2,3},{3,4},{4,5},{5,6},{6,7},{7,0},{8,9},{9,10},{10,1... | collective-permute-start | bytes 1376264 | tf_op jit(solution)/shard_map/ppermute | solution.py:16
  112.5 172.4 %reduce-scatter.6.cloned.1.call-start = ((), (), s32[]{:S(2)}) async-start(), calls=%async_computation.9 | async-start | bytes 4128768 | tf_op jit(solution)/shard_map/reduce_scatter | solution.py:139
  156.4 47.2 %copy-start.6 = (s32[32]{0:T(128)S(1)}, s32[32]{0:T(128)}, u32[]{:S(2)}) copy-start(s32[32]{0:T(128)} %param.21) | copy-start | bytes 388
  156.4 47.3 %copy-start.4 = (f32[512]{0:T(512)S(1)}, f32[512]{0:T(512)}, u32[]{:S(2)}) copy-start(f32[512]{0:T(512)} %param.23) | copy-start | bytes 6148
  156.5 47.5 %copy-start.7 = (s32[16]{0:T(128)S(1)}, s32[16]{0:T(128)}, u32[]{:S(2)}) copy-start(s32[16]{0:T(128)} %param.22) | copy-start | bytes 196
  156.5 51.5 %copy-start.2 = (bf16[256,1024]{1,0:T(8,128)(2,1)S(1)}, bf16[256,1024]{1,0:T(8,128)(2,1)}, u32[]{:S(2)}) copy-start(bf16[256,1024]{1,0:T(8,128)(2,1)} %param.12) | copy-start | bytes 1572868
  204.8 28.4 %all-to-all-start.1 = ((bf16[2,4,8]{2,0,1:T(2,128)(2,1)}), bf16[2,4,8]{2,0,1:T(2,128)(2,1)S(1)}, u32[]{:S(2)}, u32[]{:S(2)}) async-start(bf16[2,4,8]{2,0,1:T(2,128)(2,1)} %copy.38), calls=%async_computation.2 | async-start | bytes 4096 | tf_op jit(solution)/shard_map/all_to_all | solution.py:49
  233.2 11.6 %all-to-all-start.2 = ((bf16[2,32,3584]{2,0,1:T(2,128)(2,1)}), bf16[2,32,3584]{2,0,1:T(2,128)(2,1)S(1)}, u32[]{:S(2)}, u32[]{:S(2)}) async-start(bf16[2,32,3584]{2,0,1:T(2,128)(2,1)} %copy.40), calls=%async_computation.4 | async-start | bytes 917504 | tf_op jit(solution)/shard_map/all_to_all | solution.py:47
  236.7 116.7 %all-gather.11.cloned.1.call-start = ((), (), s32[]{:S(2)}) async-start(), calls=%async_computation.11 | async-start | bytes 4128768 | tf_op jit(solution)/shard_map/all_gather | solution.py:148
  287.1 162.9 %reduce-scatter.10.cloned.1.call-start = ((), (), s32[]{:S(2)}) async-start(), calls=%async_computation.12 | async-start | bytes 11468800
  374.8 80.6 %copy-start.1 = (bf16[32,3584]{1,0:T(8,128)(2,1)S(1)}, bf16[32,3584]{1,0:T(8,128)(2,1)}, u32[]{:S(2)}) copy-start(bf16[32,3584]{1,0:T(8,128)(2,1)} %param.15) | copy-start | bytes 688132
Sparse Core Ops, SparseCore 0:
  10.4 62.3 all-gather.4
  74.4 59.0 all-gather.6
  135.0 58.7 all-gather.8
  374.9 75.0 reduce-scatter.9
Sparse Core Ops, SparseCore 1:
  112.6 67.1 reduce-scatter.7
  203.8 81.1 reduce-scatter.5
  287.6 65.8 all-gather.10
